TPU v7x, 32 devices: a whole 2x2x4 slice. The times are simulated.
32 devices in a mesh: group: 2 (over x), ctx: 16 (over z, y, core).
Axes of the slice: x: 2, y: 2, z: 4, core: 2. Of those that a mesh axis runs over, the one named last changes fastest.
Arguments:
- queries: bfloat16 [4, 1536, 1024], P('group', 'ctx'), parts along dimension 0, may hold values from -6 to 6
- keys: bfloat16 [4, 1536, 128], P('group', 'ctx'), parts along dimension 0, may hold values from -6 to 6
- values: bfloat16 [4, 1536, 128], P('group', 'ctx'), parts along dimension 0, may hold values from -6 to 6
- lengths: int32 [4], P('group'), parts along dimension 0, may hold values from 384 to 1536, as said below
Outputs:
- attended: bfloat16 [4, 1536, 1024], P('group', 'ctx'), parts along dimension 0
There are 2 independent parts, one for each index of `group`. A program takes and returns all parts, laid end to end along the dimension named above; each array names one. Nothing has to cross between parts.
Inputs may be any that keep to these rules, and one draw needn't show every extreme that they name: `lengths`: in every draw at least one sequence has all 1536 positions real.
All inputs are finite; a program needn't handle non-finite values.
Results may differ from a plain program's by a relative error of at most 0.0045.
Values may be sent and summed in bfloat16 or wider, within the bound.
A program may use at most 64 MiB of HBM per device.

v0:
```python
import jax
import jax.numpy as jnp
from jax import lax
from jax.sharding import PartitionSpec as P

NEG_FILL = -1e30


def local(queries, keys, values, lengths):
    seq_count, row_count, width = queries.shape
    head_size = keys.shape[2]
    head_count = width // head_size
    my_index = lax.axis_index("ctx")
    row_ids = jnp.arange(row_count, dtype=jnp.int32)
    query_rows, key_rows, value_rows = (queries, keys, values)

    def position_of(source, offset):
        return source * row_count + offset

    query_pos = position_of(my_index, row_ids)
    query_heads = query_rows.reshape(seq_count, row_count, head_count, head_size)
    score_scale = head_size ** (-0.5)

    def update(state_now, key_piece, value_piece, key_pos):
        running_max, running_sum, numer_acc = state_now
        scores = (
            jnp.einsum("sqhd,skd->shqk", query_heads, key_piece, preferred_element_type=jnp.float32)
            * score_scale
        )
        visible = (key_pos[None, None, :] <= query_pos[None, :, None]) & (
            key_pos[None, None, :] < lengths[:, None, None]
        )
        visible = visible[:, None]
        scores = jnp.where(visible, scores, NEG_FILL)
        new_max = jnp.maximum(running_max, jnp.max(scores, axis=-1))
        weights = jnp.where(visible, jnp.exp(scores - new_max[..., None]), 0.0)
        factor = jnp.exp(running_max - new_max)
        running_sum = running_sum * factor + jnp.sum(weights, axis=-1)
        numer_acc = numer_acc * factor[..., None] + jnp.einsum(
            "shqk,skd->shqd",
            weights.astype(jnp.bfloat16),
            value_piece,
            preferred_element_type=jnp.float32,
        )
        return (new_max, running_sum, numer_acc)

    def absorb_block(state_now, key_piece, value_piece, first_row):
        piece_len = key_piece.shape[1]
        flat_idx = first_row + jnp.arange(piece_len, dtype=jnp.int32)
        key_pos = position_of(flat_idx // row_count, flat_idx % row_count)
        return update(state_now, key_piece, value_piece, key_pos)

    def absorb(state_now, pieces, first_row):
        key_piece, value_piece = pieces
        piece_len = key_piece.shape[1]
        block_len = 1
        for cand in range(1, min(piece_len, 1024) + 1):
            if piece_len % cand == 0:
                block_len = cand
        if block_len == piece_len:
            return absorb_block(state_now, key_piece, value_piece, first_row)
        block_count = piece_len // block_len
        key_blocks = jnp.moveaxis(
            key_piece.reshape(seq_count, block_count, block_len, head_size), 1, 0
        )
        value_blocks = jnp.moveaxis(
            value_piece.reshape(seq_count, block_count, block_len, head_size), 1, 0
        )

        def step(carry, inputs):
            key_blk, value_blk, blk_idx = inputs
            return (absorb_block(carry, key_blk, value_blk, first_row + blk_idx * block_len), None)

        final_state, unused = lax.scan(
            step, state_now, (key_blocks, value_blocks, jnp.arange(block_count, dtype=jnp.int32))
        )
        return final_state

    start_state = (
        jnp.full((seq_count, head_count, row_count), NEG_FILL, jnp.float32),
        jnp.zeros((seq_count, head_count, row_count), jnp.float32),
        jnp.zeros((seq_count, head_count, row_count, head_size), jnp.float32),
    )
    running_max, running_sum, numer_acc = absorb(
        start_state,
        (
            lax.all_gather(key_rows, "ctx", axis=1, tiled=True),
            lax.all_gather(value_rows, "ctx", axis=1, tiled=True),
        ),
        jnp.int32(0),
    )
    is_valid = query_pos[None, :] < lengths[:, None]
    divisor = jnp.where(is_valid[:, None, :], running_sum, 1.0)
    result = jnp.where(is_valid[:, None, :, None], numer_acc / divisor[..., None], 0.0)
    result = result.transpose(0, 2, 1, 3).reshape(seq_count, row_count, width).astype(jnp.bfloat16)
    return result


def solution(mesh):
    in_specs = (
        P("group", "ctx", None),
        P("group", "ctx", None),
        P("group", "ctx", None),
        P("group"),
    )
    out_specs = P("group", "ctx", None)
    return jax.shard_map(local, mesh=mesh, in_specs=in_specs, out_specs=out_specs, check_vma=False)
```

profile of v0, /device:TPU:0, one launch (start us, length us, event | category | flops | bytes accessed | tf_op | source)
XLA Modules:
  0.0 69.9 jit_solution(11227820105936676060)
XLA Ops:
  0.0 0.0 copy-start
  0.0 25.8 %all_gather.6 = bf16[2,1536,128]{2,1,0:T(8,128)(2,1)S(1)} all-gather(bf16[2,96,128]{2,1,0:T(8,128)(2,1)} %param.7), channel_id=1, replica_groups=mesh['group'=2,'ctx'=16] {'ctx'}, dimensions={1}, use_global_device_ids=true | all-gather | bytes 835584 | tf_op jit(solution)/shard_map/all_gather | solution.py:87
  25.8 19.8 %all_gather.7 = bf16[2,1536,128]{2,1,0:T(8,128)(2,1)S(1)} all-gather(bf16[2,96,128]{2,1,0:T(8,128)(2,1)} %param.8), channel_id=1, replica_groups=mesh['group'=2,'ctx'=16] {'ctx'}, dimensions={1}, use_global_device_ids=true | all-gather | bytes 835584 | tf_op jit(solution)/shard_map/all_gather | solution.py:88
  45.7 0.0 copy-done
  45.7 0.1 copy_bitcast_fusion.1
  45.8 22.3 %while.17 = (s32[]{:T(128)}, f32[2,8,96]{2,1,0:T(8,128)S(1)}, f32[2,8,96]{2,1,0:T(8,128)S(1)}, f32[2,8,96,128]{3,2,1,0:T(8,128)S(1)}, s32[2]{0:T(128)S(1)}, /*in...) while((s32[]{:T(128)}, f32[2,8,96]{2,1,0:T(8,128)S(1)}, ...), condition=%wide.region_3.4_spmd.clone, body=%wide.region_0.3_spmd.clone.sunk | while | flops 620147072 | bytes 36635604 | solution.py:74
  45.8 0.7 dynamic_slice.38
  47.2 0.1 broadcast_compare_fusion.6
  47.3 0.7 %broadcast_compare_fusion.5 = pred[2,768]{1,0:T(4,128)(4,1)S(1)} fusion(s32[768]{0:T(1024)S(1)} %fusion.44, s32[2]{0:T(128)} %get-tuple-element.306), kind=kLoop, calls=%fused_computation.32.clone.1 | loop fusion | flops 1536 | bytes 4616 | tf_op jit(solution)/shard_map/while/body/eval_jaxpr/lt | solution.py:31
  48.0 0.1 broadcast_and_fusion.2
  48.1 3.0 %fusion.45 = (f32[2,8,96]{2,1,0:T(8,128)S(1)}, f32[2,768,96,8]{1,2,3,0:T(8,128)}) fusion(pred[2,96,768]{2,1,0:T(8,128)(4,1)S(1)} %broadcast_and_fusion.2, bf16[2,96,8,128]{3,1,2,0:T(8,128)(2,1)S(1)} %get-tuple-element.308, bf16[2,2,768,128]{3,2,0,1:T(8,128)(2,1)S(1)} %get-tuple-element.307, s32[]{:T(128)} %get-tuple-element.288), kind=kOutput, calls=%fused_computation.3.clone.1 | convolution fusion | flops 305527296 | bytes 5658628 | tf_op jit(solution)/shard_map/while/body/eval_jaxpr/sqhd,skd->shqk/dot_general | solution.py:27
  51.1 3.9 %fusion.46 = f32[2,8,96]{2,1,0:T(8,128)S(1)} fusion(f32[2,768,96,8]{1,2,3,0:T(8,128)} %get-tuple-element.272, f32[2,8,96]{2,1,0:T(8,128)S(1)} %select_maximum_fusion.2, pred[2,96,768]{2,1,0:T(8,128)(4,1)S(1)} %broadcast_and_fusion.2), kind=kLoop, calls=%fused_computation.5.clone.1 | loop fusion | flops 5896704 | bytes 4878336 | tf_op jit(solution)/shard_map/while/body/eval_jaxpr/reduce_sum | solution.py:38
  55.1 0.0 copy-done.1
  55.1 1.7 %fusion.48 = f32[2,8,96,128]{3,2,1,0:T(8,128)S(1)} fusion(f32[2,768,96,8]{1,2,3,0:T(8,128)S(1)} %copy-done.1, f32[2,8,96]{2,1,0:T(8,128)S(1)} %select_maximum_fusion.2, pred[2,96,768]{2,1,0:T(8,128)(4,1)S(1)} %broadcast_and_fusion.2, f32[2,8,96,128]{3,2,1,0:T(8,128)S(1)} %get-tuple-element.291, bf16[2,2,768,128]{3,2,0,1:T(8,128)(2,1)S(1)} %get-tuple-element.309, ...), kind=kOutput, calls=%fused_computation.8.clone.1 | convolution fusion | flops 308477952 | bytes 6848517 | tf_op jit(solution)/shard_map/while/body/eval_jaxpr/shqk,skd->shqd/dot_general | solution.py:39
  56.9 0.7 dynamic_slice.38
  58.3 0.1 broadcast_compare_fusion.6
  58.4 0.7 %broadcast_compare_fusion.5 = pred[2,768]{1,0:T(4,128)(4,1)S(1)} fusion(s32[768]{0:T(1024)S(1)} %fusion.44, s32[2]{0:T(128)} %get-tuple-element.306), kind=kLoop, calls=%fused_computation.32.clone.1 | loop fusion | flops 1536 | bytes 4616 | tf_op jit(solution)/shard_map/while/body/eval_jaxpr/lt | solution.py:31
  59.2 0.1 broadcast_and_fusion.2
  59.2 3.0 %fusion.45 = (f32[2,8,96]{2,1,0:T(8,128)S(1)}, f32[2,768,96,8]{1,2,3,0:T(8,128)}) fusion(pred[2,96,768]{2,1,0:T(8,128)(4,1)S(1)} %broadcast_and_fusion.2, bf16[2,96,8,128]{3,1,2,0:T(8,128)(2,1)S(1)} %get-tuple-element.308, bf16[2,2,768,128]{3,2,0,1:T(8,128)(2,1)S(1)} %get-tuple-element.307, s32[]{:T(128)} %get-tuple-element.288), kind=kOutput, calls=%fused_computation.3.clone.1 | convolution fusion | flops 305527296 | bytes 5658628 | tf_op jit(solution)/shard_map/while/body/eval_jaxpr/sqhd,skd->shqk/dot_general | solution.py:27
  62.3 3.9 %fusion.46 = f32[2,8,96]{2,1,0:T(8,128)S(1)} fusion(f32[2,768,96,8]{1,2,3,0:T(8,128)} %get-tuple-element.272, f32[2,8,96]{2,1,0:T(8,128)S(1)} %select_maximum_fusion.2, pred[2,96,768]{2,1,0:T(8,128)(4,1)S(1)} %broadcast_and_fusion.2), kind=kLoop, calls=%fused_computation.5.clone.1 | loop fusion | flops 5896704 | bytes 4878336 | tf_op jit(solution)/shard_map/while/body/eval_jaxpr/reduce_sum | solution.py:38
  66.3 0.0 copy-done.1
  66.3 1.7 %fusion.48 = f32[2,8,96,128]{3,2,1,0:T(8,128)S(1)} fusion(f32[2,768,96,8]{1,2,3,0:T(8,128)S(1)} %copy-done.1, f32[2,8,96]{2,1,0:T(8,128)S(1)} %select_maximum_fusion.2, pred[2,96,768]{2,1,0:T(8,128)(4,1)S(1)} %broadcast_and_fusion.2, f32[2,8,96,128]{3,2,1,0:T(8,128)S(1)} %get-tuple-element.291, bf16[2,2,768,128]{3,2,0,1:T(8,128)(2,1)S(1)} %get-tuple-element.309, ...), kind=kOutput, calls=%fused_computation.8.clone.1 | convolution fusion | flops 308477952 | bytes 6848517 | tf_op jit(solution)/shard_map/while/body/eval_jaxpr/shqk,skd->shqd/dot_general | solution.py:39
  68.1 0.7 %broadcast_compare_fusion.2 = pred[2,96]{1,0:T(4,128)(4,1)S(1)} fusion(s32[96]{0:T(128)S(1)} %iota_add_fusion.2, s32[2]{0:T(128)} %get-tuple-element.314), kind=kLoop, calls=%fused_computation.44 | loop fusion | flops 192 | bytes 584 | tf_op jit(solution)/shard_map/lt | solution.py:92
  68.8 1.1 %copy_bitcast_fusion = bf16[2,96,1024]{2,1,0:T(8,128)(2,1)} fusion(f32[2,8,96,128]{3,2,1,0:T(8,128)S(1)} %get-tuple-element.134, f32[2,8,96]{2,1,0:T(8,128)S(1)} %broadcast_select_fusion, pred[2,96]{1,0:T(4,128)(4,1)S(1)} %broadcast_compare_fusion.2), kind=kLoop, calls=%fused_computation.40 | loop fusion | flops 589824 | bytes 1185984 | tf_op jit(solution)/shard_map/convert_element_type | solution.py:95
  (18 shorter events, 0.1 us)
Async XLA Ops:
  0.0 45.7 %copy-start = (bf16[2,96,1024]{2,1,0:T(8,128)(2,1)S(1)}, bf16[2,96,1024]{2,1,0:T(8,128)(2,1)}, u32[]{:S(2)}) copy-start(bf16[2,96,1024]{2,1,0:T(8,128)(2,1)} %param.6) | copy-start | bytes 1179652
  51.1 4.0 %copy-start.1 = (f32[2,768,96,8]{1,2,3,0:T(8,128)S(1)}, f32[2,768,96,8]{1,2,3,0:T(8,128)}, u32[]{:S(2)}) copy-start(f32[2,768,96,8]{1,2,3,0:T(8,128)} %get-tuple-element.272) | copy-start | bytes 14155780 | tf_op jit(solution)/shard_map/while
  62.3 4.0 %copy-start.1 = (f32[2,768,96,8]{1,2,3,0:T(8,128)S(1)}, f32[2,768,96,8]{1,2,3,0:T(8,128)}, u32[]{:S(2)}) copy-start(f32[2,768,96,8]{1,2,3,0:T(8,128)} %get-tuple-element.272) | copy-start | bytes 14155780 | tf_op jit(solution)/shard_map/while
where the time goes:
time: 70 us; the launch traced here: 69.9 us
  blocking collectives  45.7 us (65%)
  other arithmetic  11.6 us (17%)
  matrix products  9.59 us (14%)
  loops' own time  1.54 us (2%)
  local copies, waits for them, and re-layouts  1.42 us (2%)
    all_gather x1, blocking collectives, local(): lax.all_gather(key_rows, 'ctx', axis=1, tiled=True)  25.8 us
    all_gather x1, blocking collectives, local(): lax.all_gather(value_rows, 'ctx', axis=1, tiled=True)  19.8 us
    reduce_sum x2, other arithmetic, update(): running_sum = running_sum * factor + jnp.sum(weights, axis=-1)  7.9 us
    dot_general x2, matrix products, update(): jnp.einsum('sqhd,skd->shqk', query_heads, key_piece, preferred_element_ty...  6.09 us
    dot_general x2, matrix products, update(): jnp.einsum('shqk,skd->shqd', weights.astype(jnp.bfloat16), value_piece, p...  3.5 us
    another operation x1, loops' own time, absorb(): lax.scan(step, state_now, (key_blocks, value_blocks, jnp.arange(block_cou...  1.54 us
    lt x2, other arithmetic, update(): key_pos[None, None, :] < lengths[:, None, None]  1.46 us

commit v1 on v0

v1 whole, which is shorter than its diff:
```python
import functools
import math

import jax
import jax.numpy as jnp
from jax import lax
from jax.experimental import pallas as pl
from jax.experimental.pallas import tpu as pltpu
from jax.sharding import PartitionSpec as P

NEG_FILL = -1e30
MESH = pl.DeviceIdType.MESH
HEADS_PER_CHUNK = 4


def kernel(outer, mid, len_ref, q_hbm, k_hbm, v_hbm, o_ref, kv, qbuf, m_ref, l_ref, acc_ref,
           local_sem, recv_sem, send_z, send_y, send_c):
    seqs, heads, rows, hd = qbuf.shape
    plane = mid * 2
    group_keys = plane * rows
    scale2 = (hd ** -0.5) * math.log2(math.e)
    me = lax.axis_index("ctx")
    grp = lax.axis_index("group")
    core = lax.rem(me, 2)
    mine = lax.rem(me // 2, mid)
    o = me // plane

    def idx(oo, mm, cc):
        return (oo * mid + mm) * 2 + cc

    def peer(j):
        return lax.rem(mine + j, mid)

    def block(b):
        return kv.at[:, :, pl.ds(pl.multiple_of(b * rows, rows), rows), :]

    def rcopy(b, dev, sem):
        return pltpu.make_async_remote_copy(
            src_ref=block(b), dst_ref=block(b), send_sem=sem, recv_sem=recv_sem.at[b],
            device_id=(grp, dev), device_id_type=MESH)

    own = pl.ds(pl.multiple_of(me * rows, rows), rows)
    kv_loads = [
        pltpu.make_async_copy(k_hbm, kv.at[0, :, own, :], local_sem.at[0]),
        pltpu.make_async_copy(v_hbm, kv.at[1, :, own, :], local_sem.at[1]),
    ]
    q_loads = [
        pltpu.make_async_copy(q_hbm.at[:, :, pl.ds(h * hd, hd)], qbuf.at[:, h], local_sem.at[2 + h])
        for h in range(heads)
    ]
    for c in kv_loads:
        c.start()

    barrier = pltpu.get_barrier_semaphore()
    partner_core = idx(o, mine, 1 - core)

    def greet(dev):
        pl.semaphore_signal(barrier, inc=1, device_id=(grp, dev), device_id_type=MESH)

    for d in range(1, outer):
        greet(idx(lax.rem(o + d, outer), mine, core))
    for j in range(1, mid):
        greet(idx(o, peer(j), core))
    greet(partner_core)
    for c in q_loads:
        c.start()
    for c in kv_loads:
        c.wait()
    pl.semaphore_wait(barrier, outer - 1 + mid - 1 + 1)

    def forward(d):
        b = idx(o - d, mine, core)
        for j in range(1, mid):
            rcopy(b, idx(o, peer(j), core), send_y.at[d, j]).start()
        rcopy(b, partner_core, send_c.at[d, 0]).start()

    for d in range(1, outer):
        @pl.when(o + d < outer)
        def _():
            rcopy(me, idx(o + d, mine, core), send_z.at[d]).start()
    forward(0)

    m_ref[...] = jnp.full(m_ref.shape, NEG_FILL, jnp.float32)
    l_ref[...] = jnp.zeros(l_ref.shape, jnp.float32)
    acc_ref[...] = jnp.zeros(acc_ref.shape, jnp.float32)
    query_pos = me * rows + lax.broadcasted_iota(jnp.int32, (rows, group_keys), 0)
    key_off = lax.broadcasted_iota(jnp.int32, (rows, group_keys), 1)
    for c in q_loads:
        c.wait()

    def step(d, carry):
        for j in range(1, mid):
            b = idx(o - d, peer(j), core)
            rcopy(b, partner_core, send_c.at[d, j]).wait_recv()
            rcopy(b, partner_core, send_c.at[d, j]).start()

        @pl.when(d < o)
        def _():
            b = idx(o - d - 1, mine, core)
            rcopy(b, partner_core, send_c.at[d + 1, 0]).wait_recv()
            forward(d + 1)

        for j in range(mid):
            b = idx(o - d, peer(j), 1 - core)
            rcopy(b, partner_core, send_c.at[d, j]).wait_recv()

        first = pl.multiple_of((o - d) * group_keys, group_keys)
        keys_at = pl.ds(first, group_keys)
        hc = HEADS_PER_CHUNK
        for s in range(seqs):
            visible = (first + key_off <= query_pos) & (first + key_off < len_ref[s])
            bias = jnp.where(visible, 0.0, NEG_FILL)
            k_blk = kv[0, s, keys_at, :]
            v_blk = kv[1, s, keys_at, :]
            for h in range(0, heads, hc):
                q_blk = qbuf[s, h:h + hc].reshape(hc * rows, hd)
                sc = lax.dot_general(q_blk, k_blk, (((1,), (1,)), ((), ())),
                                     preferred_element_type=jnp.float32)
                sc = sc.reshape(hc, rows, group_keys) + bias[None]
                m_old = m_ref[s, h:h + hc]
                m_new = jnp.maximum(m_old, jnp.max(sc, axis=-1, keepdims=True))
                m_ref[s, h:h + hc] = m_new
                p = jnp.exp2((sc - m_new[:, :, :1]) * scale2)
                alpha = jnp.exp2((m_old - m_new) * scale2)
                part = p[:, :, :hd]
                for t in range(hd, group_keys, hd):
                    part = part + p[:, :, t:t + hd]
                l_ref[s, h:h + hc] = l_ref[s, h:h + hc] * alpha + part
                pv = jnp.dot(p.astype(jnp.bfloat16).reshape(hc * rows, group_keys), v_blk,
                             preferred_element_type=jnp.float32)
                acc_ref[s, h:h + hc] = acc_ref[s, h:h + hc] * alpha + pv.reshape(hc, rows, hd)
        return carry

    lax.fori_loop(0, o + 1, step, jnp.int32(0))

    pos = me * rows + lax.broadcasted_iota(jnp.int32, (rows, hd), 0)
    for s in range(seqs):
        is_valid = pos < len_ref[s]
        for h in range(heads):
            total = jnp.sum(l_ref[s, h], axis=-1, keepdims=True)
            divisor = jnp.where(is_valid, total, 1.0)
            res = jnp.where(is_valid, acc_ref[s, h] / divisor, 0.0)
            o_ref[s, :, h * hd:(h + 1) * hd] = res.astype(jnp.bfloat16)

    for d in range(1, outer):
        @pl.when(o + d < outer)
        def _():
            rcopy(me, idx(o + d, mine, core), send_z.at[d]).wait_send()

    def drain(d, carry):
        b = idx(o - d, mine, core)
        for j in range(1, mid):
            rcopy(b, partner_core, send_y.at[d, j]).wait_send()
        for j in range(mid):
            rcopy(b, partner_core, send_c.at[d, j]).wait_send()
        return carry

    lax.fori_loop(0, o + 1, drain, jnp.int32(0))


def solution(mesh):
    n = mesh.shape["ctx"]
    mid = 1
    while mid * mid * 4 * 2 <= n:
        mid *= 2
    outer = n // (2 * mid)

    def local(queries, keys, values, lengths):
        seqs, rows, width = queries.shape
        hd = keys.shape[2]
        heads = width // hd
        hbm = pl.BlockSpec(memory_space=pl.ANY)
        return pl.pallas_call(
            functools.partial(kernel, outer, mid),
            out_shape=jax.ShapeDtypeStruct(queries.shape, jnp.bfloat16),
            in_specs=[pl.BlockSpec(memory_space=pltpu.SMEM), hbm, hbm, hbm],
            out_specs=pl.BlockSpec(memory_space=pltpu.VMEM),
            scratch_shapes=[
                pltpu.VMEM((2, seqs, n * rows, hd), jnp.bfloat16),
                pltpu.VMEM((seqs, heads, rows, hd), jnp.bfloat16),
                pltpu.VMEM((seqs, heads, rows, hd), jnp.float32),
                pltpu.VMEM((seqs, heads, rows, hd), jnp.float32),
                pltpu.VMEM((seqs, heads, rows, hd), jnp.float32),
                pltpu.SemaphoreType.DMA((2 + heads,)),
                pltpu.SemaphoreType.DMA((n,)),
                pltpu.SemaphoreType.DMA((outer,)),
                pltpu.SemaphoreType.DMA((outer, mid)),
                pltpu.SemaphoreType.DMA((outer, mid)),
            ],
            compiler_params=pltpu.CompilerParams(
                collective_id=0, has_side_effects=True, vmem_limit_bytes=48 * 1024 * 1024),
        )(lengths, queries, keys, values)

    return jax.shard_map(
        local, mesh=mesh,
        in_specs=(P("group", "ctx", None), P("group", "ctx", None), P("group", "ctx", None), P("group")),
        out_specs=P("group", "ctx", None), check_vma=False)
```

time: 70 us -> 29 us (0.41)
  the two profiles are of different devices: /device:TPU:0 before, /device:TPU:31 now
where the time goes in v1:
time: 29 us; the launch traced here: 28.7 us
  Pallas kernels  24.7 us (85%)
  local copies, waits for them, and re-layouts  3.99 us (14%)
    pallas_call x1, Pallas kernels, local(): pl.pallas_call(functools.partial(kernel, outer, mid), out_shape=jax.Shape...  24.7 us
    unnamed x9, local copies, waits for them, and re-layouts  3.99 us

profile of v1, /device:TPU:31, one launch (start us, length us, event | category | flops | bytes accessed | tf_op | source)
XLA Modules:
  0.0 28.7 jit_solution(12380005563934736573)
XLA Ops:
  0.0 0.0 copy-start
  0.0 1.0 %copy-done = bf16[2,96,1024]{2,1,0:T(8,128)(2,1)S(1)} copy-done((bf16[2,96,1024]{2,1,0:T(8,128)(2,1)S(1)}, bf16[2,96,1024]{2,1,0:T(8,128)(2,1)}, u32[]{:S(2)}) %copy-start) | copy-done | bytes 393240
  1.0 0.0 copy-start.1
  1.0 0.8 %copy-done.1 = bf16[2,96,128]{2,1,0:T(8,128)(2,1)S(1)} copy-done((bf16[2,96,128]{2,1,0:T(8,128)(2,1)S(1)}, bf16[2,96,128]{2,1,0:T(8,128)(2,1)}, u32[]{:S(2)}) %copy-start.1) | copy-done | bytes 49176
  1.8 0.0 copy-start.2
  1.8 0.8 %copy-done.2 = bf16[2,96,128]{2,1,0:T(8,128)(2,1)S(1)} copy-done((bf16[2,96,128]{2,1,0:T(8,128)(2,1)S(1)}, bf16[2,96,128]{2,1,0:T(8,128)(2,1)}, u32[]{:S(2)}) %copy-start.2) | copy-done | bytes 49176
  2.6 0.0 copy-start.3
  2.6 0.7 %copy-done.3 = s32[2]{0:T(128)S(1)} copy-done((s32[2]{0:T(128)S(1)}, s32[2]{0:T(128)}, u32[]{:S(2)}) %copy-start.3) | copy-done | bytes 32
  3.3 24.7 %shard_map.46 = bf16[2,96,1024]{2,1,0:T(8,128)(2,1)S(1)} custom-call(s32[2]{0:T(128)S(1)} %copy-done.3, bf16[2,96,1024]{2,1,0:T(8,128)(2,1)S(1)} %copy-done, bf16[2,96,128]{2,1,0:T(8,128)(2,1)S(1)} %copy-done.1, bf16[2,96,128]{2,1,0:T(8,128)(2,1)S(1)} %copy-done.2), custom_call_target="tpu_custom_call" | custom-call | tf_op jit(solution)/shard_map/pallas_call | solution.py:173
  28.0 0.7 %copy.6 = bf16[2,96,1024]{2,1,0:T(8,128)(2,1)} copy(bf16[2,96,1024]{2,1,0:T(8,128)(2,1)S(1)} %shard_map.46) | data formatting | bytes 786432
Async XLA Ops:
  0.0 1.0 %copy-start = (bf16[2,96,1024]{2,1,0:T(8,128)(2,1)S(1)}, bf16[2,96,1024]{2,1,0:T(8,128)(2,1)}, u32[]{:S(2)}) copy-start(bf16[2,96,1024]{2,1,0:T(8,128)(2,1)} %q_hbm.1) | copy-start | bytes 1179652
  1.0 0.8 %copy-start.1 = (bf16[2,96,128]{2,1,0:T(8,128)(2,1)S(1)}, bf16[2,96,128]{2,1,0:T(8,128)(2,1)}, u32[]{:S(2)}) copy-start(bf16[2,96,128]{2,1,0:T(8,128)(2,1)} %k_hbm.1) | copy-start | bytes 147460
  1.8 0.8 %copy-start.2 = (bf16[2,96,128]{2,1,0:T(8,128)(2,1)S(1)}, bf16[2,96,128]{2,1,0:T(8,128)(2,1)}, u32[]{:S(2)}) copy-start(bf16[2,96,128]{2,1,0:T(8,128)(2,1)} %v_hbm.1) | copy-start | bytes 147460
  2.6 0.7 %copy-start.3 = (s32[2]{0:T(128)S(1)}, s32[2]{0:T(128)}, u32[]{:S(2)}) copy-start(s32[2]{0:T(128)} %len_ref.1) | copy-start | bytes 28

commit v2 on v1

v2 whole, which is shorter than its diff:
```python
import functools
import math

import jax
import jax.numpy as jnp
from jax import lax
from jax.experimental import pallas as pl
from jax.experimental.pallas import tpu as pltpu
from jax.sharding import PartitionSpec as P

NEG_FILL = -1e30
MESH = pl.DeviceIdType.MESH
HEADS_PER_CHUNK = 8


def kernel(outer, mid, len_hbm, q_hbm, k_hbm, v_hbm, o_ref, kv, qbuf, m_ref, l_ref, acc_ref, len_ref,
           local_sem, recv_sem, send_z, send_y, send_c):
    seqs, heads, rows, hd = qbuf.shape
    plane = mid * 2
    group_keys = plane * rows
    scale2 = (hd ** -0.5) * math.log2(math.e)
    me = lax.axis_index("ctx")
    grp = lax.axis_index("group")
    core = lax.rem(me, 2)
    mine = lax.rem(me // 2, mid)
    o = me // plane

    def idx(oo, mm, cc):
        return (oo * mid + mm) * 2 + cc

    def peer(j):
        return lax.rem(mine + j, mid)

    def unit(b, s):
        return kv.at[:, s, pl.ds(pl.multiple_of(b * rows, rows), rows), :]

    def rcopy(b, s, dev, sem):
        return pltpu.make_async_remote_copy(
            src_ref=unit(b, s), dst_ref=unit(b, s), send_sem=sem, recv_sem=recv_sem.at[b, s],
            device_id=(grp, dev), device_id_type=MESH)

    own = pl.ds(pl.multiple_of(me * rows, rows), rows)
    kv_loads = [
        pltpu.make_async_copy(k_hbm, kv.at[0, :, own, :], local_sem.at[0]),
        pltpu.make_async_copy(v_hbm, kv.at[1, :, own, :], local_sem.at[1]),
    ]
    q_loads = [
        pltpu.make_async_copy(q_hbm.at[:, :, pl.ds(h * hd, hd)], qbuf.at[:, h], local_sem.at[2 + h])
        for h in range(heads)
    ]
    len_load = pltpu.make_async_copy(len_hbm, len_ref, local_sem.at[2 + heads])
    for c in kv_loads:
        c.start()
    len_load.start()

    barrier = pltpu.get_barrier_semaphore()
    partner_core = idx(o, mine, 1 - core)

    def greet(dev):
        pl.semaphore_signal(barrier, inc=1, device_id=(grp, dev), device_id_type=MESH)

    has_up = o < outer - 1
    has_down = o > 0
    above = idx(jnp.minimum(o + 1, outer - 1), mine, core)
    below = idx(jnp.maximum(o - 1, 0), mine, core)

    @pl.when(has_up)
    def _():
        greet(above)

    @pl.when(has_down)
    def _():
        greet(below)

    for j in range(1, mid):
        greet(idx(o, peer(j), core))
    greet(partner_core)
    for c in q_loads:
        c.start()
    for c in kv_loads:
        c.wait()
    pl.semaphore_wait(barrier, mid + has_up.astype(jnp.int32) + has_down.astype(jnp.int32))

    def forward(u):
        d, s = u // seqs, lax.rem(u, seqs)
        b = idx(o - d, mine, core)

        @pl.when(has_up)
        def _():
            rcopy(b, s, above, send_z.at[u]).start()

        for j in range(1, mid):
            rcopy(b, s, idx(o, peer(j), core), send_y.at[u, j]).start()
        rcopy(b, s, partner_core, send_c.at[u, 0]).start()

    for u in range(seqs):
        forward(u)

    m_ref[...] = jnp.full(m_ref.shape, NEG_FILL, jnp.float32)
    l_ref[...] = jnp.zeros(l_ref.shape, jnp.float32)
    acc_ref[...] = jnp.zeros(acc_ref.shape, jnp.float32)
    query_pos = me * rows + lax.broadcasted_iota(jnp.int32, (rows, group_keys), 0)
    key_off = lax.broadcasted_iota(jnp.int32, (rows, group_keys), 1)
    for c in q_loads:
        c.wait()
    len_load.wait()

    def attend(u):
        d, s = u // seqs, lax.rem(u, seqs)
        for j in range(mid):
            rcopy(idx(o - d, peer(j), 1 - core), s, partner_core, send_c.at[u, j]).wait_recv()
        first = pl.multiple_of((o - d) * group_keys, group_keys)
        keys_at = pl.ds(first, group_keys)
        hc = HEADS_PER_CHUNK
        visible = (first + key_off <= query_pos) & (first + key_off < len_ref[s])
        bias = jnp.where(visible, 0.0, NEG_FILL)
        k_blk = kv[0, s, keys_at, :]
        v_blk = kv[1, s, keys_at, :]
        for h in range(0, heads, hc):
            hs = pl.ds(h, hc)
            q_blk = qbuf[s, hs].reshape(hc * rows, hd)
            sc = lax.dot_general(q_blk, k_blk, (((1,), (1,)), ((), ())),
                                 preferred_element_type=jnp.float32)
            sc = sc.reshape(hc, rows, group_keys) + bias[None]
            m_old = m_ref[s, hs]
            m_new = jnp.maximum(m_old, jnp.max(sc, axis=-1, keepdims=True))
            m_ref[s, hs] = m_new
            p = jnp.exp2((sc - m_new[:, :, :1]) * scale2)
            alpha = jnp.exp2((m_old - m_new) * scale2)
            part = p[:, :, :hd]
            for t in range(hd, group_keys, hd):
                part = part + p[:, :, t:t + hd]
            l_ref[s, hs] = l_ref[s, hs] * alpha + part
            pv = jnp.dot(p.astype(jnp.bfloat16).reshape(hc * rows, group_keys), v_blk,
                         preferred_element_type=jnp.float32)
            acc_ref[s, hs] = acc_ref[s, hs] * alpha + pv.reshape(hc, rows, hd)

    units = (o + 1) * seqs

    def step(u, carry):
        @pl.when(u + seqs < units)
        def _():
            w = u + seqs
            rcopy(idx(o - w // seqs, mine, core), lax.rem(w, seqs), partner_core,
                  send_c.at[w, 0]).wait_recv()
            forward(w)

        @pl.when(u < units)
        def _():
            for j in range(1, mid):
                b, s = idx(o - u // seqs, peer(j), core), lax.rem(u, seqs)
                rcopy(b, s, partner_core, send_c.at[u, j]).wait_recv()
                rcopy(b, s, partner_core, send_c.at[u, j]).start()

        @pl.when(u > 0)
        def _():
            attend(u - 1)

        return carry

    lax.fori_loop(0, units + 1, step, jnp.int32(0))

    pos = me * rows + lax.broadcasted_iota(jnp.int32, (rows, hd), 0)
    for s in range(seqs):
        is_valid = pos < len_ref[s]
        for h in range(heads):
            total = jnp.sum(l_ref[s, h], axis=-1, keepdims=True)
            divisor = jnp.where(is_valid, total, 1.0)
            res = jnp.where(is_valid, acc_ref[s, h] / divisor, 0.0)
            o_ref[s, :, h * hd:(h + 1) * hd] = res.astype(jnp.bfloat16)

    def drain(u, carry):
        b, s = idx(o - u // seqs, mine, core), lax.rem(u, seqs)

        @pl.when(has_up)
        def _():
            rcopy(b, s, above, send_z.at[u]).wait_send()

        for j in range(1, mid):
            rcopy(b, s, partner_core, send_y.at[u, j]).wait_send()
        for j in range(mid):
            rcopy(b, s, partner_core, send_c.at[u, j]).wait_send()
        return carry

    lax.fori_loop(0, units, drain, jnp.int32(0))


def solution(mesh):
    n = mesh.shape["ctx"]
    mid = 1
    while mid * mid * 4 * 2 <= n:
        mid *= 2
    outer = n // (2 * mid)

    def local(queries, keys, values, lengths):
        seqs, rows, width = queries.shape
        hd = keys.shape[2]
        heads = width // hd
        queries, keys, values, lengths = (
            pltpu.with_memory_space_constraint(x, pltpu.HBM) for x in (queries, keys, values, lengths))
        hbm = pl.BlockSpec(memory_space=pltpu.HBM)
        return pl.pallas_call(
            functools.partial(kernel, outer, mid),
            out_shape=jax.ShapeDtypeStruct(queries.shape, jnp.bfloat16),
            in_specs=[hbm, hbm, hbm, hbm],
            out_specs=pl.BlockSpec(memory_space=pltpu.VMEM),
            scratch_shapes=[
                pltpu.VMEM((2, seqs, n * rows, hd), jnp.bfloat16),
                pltpu.VMEM((seqs, heads, rows, hd), jnp.bfloat16),
                pltpu.VMEM((seqs, heads, rows, hd), jnp.float32),
                pltpu.VMEM((seqs, heads, rows, hd), jnp.float32),
                pltpu.VMEM((seqs, heads, rows, hd), jnp.float32),
                pltpu.SMEM((seqs,), jnp.int32),
                pltpu.SemaphoreType.DMA((3 + heads,)),
                pltpu.SemaphoreType.DMA((n, seqs)),
                pltpu.SemaphoreType.DMA((outer * seqs,)),
                pltpu.SemaphoreType.DMA((outer * seqs, mid)),
                pltpu.SemaphoreType.DMA((outer * seqs, mid)),
            ],
            compiler_params=pltpu.CompilerParams(
                collective_id=0, has_side_effects=True, vmem_limit_bytes=48 * 1024 * 1024),
        )(lengths, queries, keys, values)

    return jax.shard_map(
        local, mesh=mesh,
        in_specs=(P("group", "ctx", None), P("group", "ctx", None), P("group", "ctx", None), P("group")),
        out_specs=P("group", "ctx", None), check_vma=False)
```

time: 29 us -> 18.9 us (0.65)
  the two profiles are of different devices: /device:TPU:31 before, /device:TPU:25 now
where the time goes in v2:
time: 18.9 us; the launch traced here: 18.7 us
  Pallas kernels  18 us (95%)
  local copies, waits for them, and re-layouts  0.75 us (4%)
    pallas_call x1, Pallas kernels, local(): pl.pallas_call(functools.partial(kernel, outer, mid), out_shape=jax.Shape...  18 us
    unnamed x1, local copies, waits for them, and re-layouts  0.75 us

profile of v2, /device:TPU:25, one launch (start us, length us, event | category | flops | bytes accessed | tf_op | source)
XLA Modules:
  0.0 18.7 jit_solution(17525970365632347391)
XLA Ops:
  0.0 18.0 %shard_map.46 = bf16[2,96,1024]{2,1,0:T(8,128)(2,1)S(1)} custom-call(s32[2]{0:T(128)} %len_hbm.1, bf16[2,96,1024]{2,1,0:T(8,128)(2,1)} %q_hbm.1, bf16[2,96,128]{2,1,0:T(8,128)(2,1)} %k_hbm.1, bf16[2,96,128]{2,1,0:T(8,128)(2,1)} %v_hbm.1), custom_call_target="tpu_custom_call" | custom-call | tf_op jit(solution)/shard_map/pallas_call | solution.py:202
  18.0 0.7 %copy.6 = bf16[2,96,1024]{2,1,0:T(8,128)(2,1)} copy(bf16[2,96,1024]{2,1,0:T(8,128)(2,1)S(1)} %shard_map.46) | data formatting | bytes 786432

commit v3 on v2

--- a/solution.py
+++ b/solution.py
@@ -14,7 +14,7 @@
 
 
 def kernel(outer, mid, len_hbm, q_hbm, k_hbm, v_hbm, o_ref, kv, qbuf, m_ref, l_ref, acc_ref, len_ref,
-           local_sem, recv_sem, send_z, send_y, send_c):
+           local_sem, recv_sem, send_z, send_y, send_c, send_x):
     seqs, heads, rows, hd = qbuf.shape
     plane = mid * 2
     group_keys = plane * rows
@@ -81,6 +81,11 @@
         c.wait()
     pl.semaphore_wait(barrier, mid + has_up.astype(jnp.int32) + has_down.astype(jnp.int32))
 
+    units = (o + 1) * seqs
+
+    def crosses(u, j):
+        return (u < units - 1) | (o == 0) | (j != mid - 1)
+
     def forward(u):
         d, s = u // seqs, lax.rem(u, seqs)
         b = idx(o - d, mine, core)
@@ -90,7 +95,10 @@
             rcopy(b, s, above, send_z.at[u]).start()
 
         for j in range(1, mid):
-            rcopy(b, s, idx(o, peer(j), core), send_y.at[u, j]).start()
+            @pl.when(crosses(u, j))
+            def _():
+                rcopy(b, s, idx(o, peer(j), core), send_y.at[u, j]).start()
+
         rcopy(b, s, partner_core, send_c.at[u, 0]).start()
 
     for u in range(seqs):
@@ -116,26 +124,28 @@
         bias = jnp.where(visible, 0.0, NEG_FILL)
         k_blk = kv[0, s, keys_at, :]
         v_blk = kv[1, s, keys_at, :]
-        for h in range(0, heads, hc):
-            hs = pl.ds(h, hc)
-            q_blk = qbuf[s, hs].reshape(hc * rows, hd)
-            sc = lax.dot_general(q_blk, k_blk, (((1,), (1,)), ((), ())),
-                                 preferred_element_type=jnp.float32)
-            sc = sc.reshape(hc, rows, group_keys) + bias[None]
-            m_old = m_ref[s, hs]
-            m_new = jnp.maximum(m_old, jnp.max(sc, axis=-1, keepdims=True))
+        chunks = [pl.ds(h, hc) for h in range(0, heads, hc)]
+        tiles = [slice(t, t + hd) for t in range(0, group_keys, hd)]
+        state = [(m_ref[s, hs], l_ref[s, hs], acc_ref[s, hs]) for hs in chunks]
+        scores = [
+            lax.dot_general(qbuf[s, hs].reshape(hc * rows, hd), k_blk, (((1,), (1,)), ((), ())),
+                            preferred_element_type=jnp.float32) for hs in chunks]
+        done = []
+        for sc, (m_old, l_old, acc_old) in zip(scores, state):
+            sc = sc.reshape(hc, rows, group_keys)
+            parts = [sc[:, :, t] + bias[None, :, t] for t in tiles]
+            top = functools.reduce(jnp.maximum, parts)
+            m_new = jnp.maximum(m_old, jnp.max(top, axis=-1, keepdims=True))
+            parts = [jnp.exp2((x - m_new) * scale2) for x in parts]
+            alpha = jnp.exp2((m_old - m_new) * scale2)
+            l_new = l_old * alpha + functools.reduce(jnp.add, parts)
+            p = jnp.concatenate([x.astype(jnp.bfloat16) for x in parts], axis=-1)
+            pv = jnp.dot(p.reshape(hc * rows, group_keys), v_blk, preferred_element_type=jnp.float32)
+            done.append((m_new, l_new, acc_old * alpha + pv.reshape(hc, rows, hd)))
+        for hs, (m_new, l_new, acc_new) in zip(chunks, done):
             m_ref[s, hs] = m_new
-            p = jnp.exp2((sc - m_new[:, :, :1]) * scale2)
-            alpha = jnp.exp2((m_old - m_new) * scale2)
-            part = p[:, :, :hd]
-            for t in range(hd, group_keys, hd):
-                part = part + p[:, :, t:t + hd]
-            l_ref[s, hs] = l_ref[s, hs] * alpha + part
-            pv = jnp.dot(p.astype(jnp.bfloat16).reshape(hc * rows, group_keys), v_blk,
-                         preferred_element_type=jnp.float32)
-            acc_ref[s, hs] = acc_ref[s, hs] * alpha + pv.reshape(hc, rows, hd)
-
-    units = (o + 1) * seqs
+            l_ref[s, hs] = l_new
+            acc_ref[s, hs] = acc_new
 
     def step(u, carry):
         @pl.when(u + seqs < units)
@@ -150,6 +160,11 @@
             for j in range(1, mid):
                 b, s = idx(o - u // seqs, peer(j), core), lax.rem(u, seqs)
                 rcopy(b, s, partner_core, send_c.at[u, j]).wait_recv()
+                if j == 1:
+                    @pl.when((u == units - 1) & has_up)
+                    def _():
+                        rcopy(b, s, above, send_x.at[0]).start()
+
                 rcopy(b, s, partner_core, send_c.at[u, j]).start()
 
         @pl.when(u > 0)
@@ -177,12 +192,20 @@
             rcopy(b, s, above, send_z.at[u]).wait_send()
 
         for j in range(1, mid):
-            rcopy(b, s, partner_core, send_y.at[u, j]).wait_send()
+            @pl.when(crosses(u, j))
+            def _():
+                rcopy(b, s, partner_core, send_y.at[u, j]).wait_send()
+
         for j in range(mid):
             rcopy(b, s, partner_core, send_c.at[u, j]).wait_send()
         return carry
 
     lax.fori_loop(0, units, drain, jnp.int32(0))
+
+    if mid > 1:
+        @pl.when(has_up)
+        def _():
+            rcopy(idx(0, peer(1), core), seqs - 1, above, send_x.at[0]).wait_send()
 
 
 def solution(mesh):
@@ -216,6 +239,7 @@
                 pltpu.SemaphoreType.DMA((outer * seqs,)),
                 pltpu.SemaphoreType.DMA((outer * seqs, mid)),
                 pltpu.SemaphoreType.DMA((outer * seqs, mid)),
+                pltpu.SemaphoreType.DMA((1,)),
             ],
             compiler_params=pltpu.CompilerParams(
                 collective_id=0, has_side_effects=True, vmem_limit_bytes=48 * 1024 * 1024),

time: 18.9 us -> 18 us (0.952)
  Pallas kernels: 18 us -> 17 us
    pallas_call x1, Pallas kernels: 18 us -> 17 us  [local(): pl.pallas_call(functools.partial(kernel, outer, mid), out_shape=jax.Shape...]
where the time goes in v3:
time: 18 us; the launch traced here: 17.8 us
  Pallas kernels  17 us (94%)
  local copies, waits for them, and re-layouts  0.75 us (4%)
    pallas_call x1, Pallas kernels, local(): pl.pallas_call(functools.partial(kernel, outer, mid), out_shape=jax.Shape...  17 us
    unnamed x1, local copies, waits for them, and re-layouts  0.75 us

profile of v3, /device:TPU:25, one launch (start us, length us, event | category | flops | bytes accessed | tf_op | source)
XLA Modules:
  0.0 17.8 jit_solution(13619257684492575042)
XLA Ops:
  0.0 17.0 %shard_map.46 = bf16[2,96,1024]{2,1,0:T(8,128)(2,1)S(1)} custom-call(s32[2]{0:T(128)} %len_hbm.1, bf16[2,96,1024]{2,1,0:T(8,128)(2,1)} %q_hbm.1, bf16[2,96,128]{2,1,0:T(8,128)(2,1)} %k_hbm.1, bf16[2,96,128]{2,1,0:T(8,128)(2,1)} %v_hbm.1), custom_call_target="tpu_custom_call" | custom-call | tf_op jit(solution)/shard_map/pallas_call | solution.py:225
  17.1 0.7 %copy.6 = bf16[2,96,1024]{2,1,0:T(8,128)(2,1)} copy(bf16[2,96,1024]{2,1,0:T(8,128)(2,1)S(1)} %shard_map.46) | data formatting | bytes 786432

commit v4 on v3

--- a/solution.py
+++ b/solution.py
@@ -11,6 +11,7 @@
 NEG_FILL = -1e30
 MESH = pl.DeviceIdType.MESH
 HEADS_PER_CHUNK = 8
+RELAY_LAG = 2
 
 
 def kernel(outer, mid, len_hbm, q_hbm, k_hbm, v_hbm, o_ref, kv, qbuf, m_ref, l_ref, acc_ref, len_ref,
@@ -90,16 +91,16 @@
         d, s = u // seqs, lax.rem(u, seqs)
         b = idx(o - d, mine, core)
 
-        @pl.when(has_up)
-        def _():
-            rcopy(b, s, above, send_z.at[u]).start()
-
         for j in range(1, mid):
             @pl.when(crosses(u, j))
             def _():
                 rcopy(b, s, idx(o, peer(j), core), send_y.at[u, j]).start()
 
         rcopy(b, s, partner_core, send_c.at[u, 0]).start()
+
+        @pl.when(has_up)
+        def _():
+            rcopy(b, s, above, send_z.at[u]).start()
 
     for u in range(seqs):
         forward(u)
@@ -147,6 +148,8 @@
             l_ref[s, hs] = l_new
             acc_ref[s, hs] = acc_new
 
+    lag = jnp.where(has_up, RELAY_LAG, 1)
+
     def step(u, carry):
         @pl.when(u + seqs < units)
         def _():
@@ -167,13 +170,13 @@
 
                 rcopy(b, s, partner_core, send_c.at[u, j]).start()
 
-        @pl.when(u > 0)
-        def _():
-            attend(u - 1)
+        @pl.when(u >= lag)
+        def _():
+            attend(u - lag)
 
         return carry
 
-    lax.fori_loop(0, units + 1, step, jnp.int32(0))
+    lax.fori_loop(0, units + lag, step, jnp.int32(0))
 
     pos = me * rows + lax.broadcasted_iota(jnp.int32, (rows, hd), 0)
     for s in range(seqs):

time: 18 us -> 17.5 us (0.972)
  Pallas kernels: 17 us -> 16.6 us
    pallas_call x1, Pallas kernels: 17 us -> 16.6 us  [local(): pl.pallas_call(functools.partial(kernel, outer, mid), out_shape=jax.Shape...]
where the time goes in v4:
time: 17.5 us; the launch traced here: 17.3 us
  Pallas kernels  16.6 us (95%)
  local copies, waits for them, and re-layouts  0.75 us (4%)
    pallas_call x1, Pallas kernels, local(): pl.pallas_call(functools.partial(kernel, outer, mid), out_shape=jax.Shape...  16.6 us
    unnamed x1, local copies, waits for them, and re-layouts  0.75 us

profile of v4, /device:TPU:25, one launch (start us, length us, event | category | flops | bytes accessed | tf_op | source)
XLA Modules:
  0.0 17.3 jit_solution(4608255617273421284)
XLA Ops:
  0.0 16.6 %shard_map.46 = bf16[2,96,1024]{2,1,0:T(8,128)(2,1)S(1)} custom-call(s32[2]{0:T(128)} %len_hbm.1, bf16[2,96,1024]{2,1,0:T(8,128)(2,1)} %q_hbm.1, bf16[2,96,128]{2,1,0:T(8,128)(2,1)} %k_hbm.1, bf16[2,96,128]{2,1,0:T(8,128)(2,1)} %v_hbm.1), custom_call_target="tpu_custom_call" | custom-call | tf_op jit(solution)/shard_map/pallas_call | solution.py:228
  16.6 0.7 %copy.6 = bf16[2,96,1024]{2,1,0:T(8,128)(2,1)} copy(bf16[2,96,1024]{2,1,0:T(8,128)(2,1)S(1)} %shard_map.46) | data formatting | bytes 786432

commit v5 on v4

--- a/solution.py
+++ b/solution.py
@@ -148,7 +148,7 @@
             l_ref[s, hs] = l_new
             acc_ref[s, hs] = acc_new
 
-    lag = jnp.where(has_up, RELAY_LAG, 1)
+    lag = jnp.where(has_up, jnp.where(o == 0, 1, RELAY_LAG), 1)
 
     def step(u, carry):
         @pl.when(u + seqs < units)

time: 17.5 us -> 17.5 us (level)
  no operation moved by 1% of the time
where the time goes in v5:
time: 17.5 us; the launch traced here: 17.3 us
  Pallas kernels  16.6 us (95%)
  local copies, waits for them, and re-layouts  0.75 us (4%)
    pallas_call x1, Pallas kernels, local(): pl.pallas_call(functools.partial(kernel, outer, mid), out_shape=jax.Shape...  16.6 us
    unnamed x1, local copies, waits for them, and re-layouts  0.75 us

profile of v5, /device:TPU:25, one launch (start us, length us, event | category | flops | bytes accessed | tf_op | source)
XLA Modules:
  0.0 17.3 jit_solution(11244464520160158534)
XLA Ops:
  0.0 16.6 %shard_map.46 = bf16[2,96,1024]{2,1,0:T(8,128)(2,1)S(1)} custom-call(s32[2]{0:T(128)} %len_hbm.1, bf16[2,96,1024]{2,1,0:T(8,128)(2,1)} %q_hbm.1, bf16[2,96,128]{2,1,0:T(8,128)(2,1)} %k_hbm.1, bf16[2,96,128]{2,1,0:T(8,128)(2,1)} %v_hbm.1), custom_call_target="tpu_custom_call" | custom-call | tf_op jit(solution)/shard_map/pallas_call | solution.py:228
  16.6 0.7 %copy.6 = bf16[2,96,1024]{2,1,0:T(8,128)(2,1)} copy(bf16[2,96,1024]{2,1,0:T(8,128)(2,1)S(1)} %shard_map.46) | data formatting | bytes 786432
